TPU v7x, 256 devices: a whole 4x4x8 slice. The times are simulated.
256 devices in a mesh: shift: 8 (over x, core), rows: 32 (over y, z).
Axes of the slice: x: 4, y: 4, z: 8, core: 2. Of those that a mesh axis runs over, the one named last changes fastest.
Arguments:
- neighbours: int32 [256, 8], P('rows'), may hold values from 0 to 255, as said below
- couplings: float32 [256, 8, 128, 128], P('rows'), may hold values from -0.01953125 to 0.01953125
- eigvectors: float32 [256, 128, 128], P('rows'), may hold values from -1 to 1, as said below
- eigvalues: float32 [256, 128], P('rows'), may hold values from -2.5 to 2.5
- start_block: float32 [32768, 128], P('rows'), may hold values from -240 to 240
Outputs:
- basis: float32 [32768, 128], P('rows')
- basis_image: float32 [32768, 128], P('rows')
- projected: float32 [128, 128], replicated
Inputs may be any that keep to these rules, and one draw needn't show every extreme that they name: Each block's 8 neighbours are distinct blocks other than itself, each within 8 blocks of it. `eigvectors`: each block's matrix has orthonormal columns up to rounding.
All inputs are finite; a program needn't handle non-finite values.
Results may differ from a plain program's by a relative error of at most 0.00025.
Values sent between devices are 32-bit elements; how exact they have to be, the bound alone decides.
A program may use at most 64 MiB of HBM per device.

v0:
```python
import jax
import jax.numpy as jnp
from jax import lax
from jax.sharding import PartitionSpec as P

SWEEPS = 3
radius = 1.0
damping = 0.8


def extended(block, sides, width):
    for axis, dim in sides:
        count = lax.axis_size(axis)
        forward = [(i, i + 1) for i in range(count - 1)]
        backward = [(target, source) for source, target in forward]
        low = lax.ppermute(
            lax.slice_in_dim(block, block.shape[dim] - width, None, axis=dim), axis, forward
        )
        high = lax.ppermute(lax.slice_in_dim(block, 0, width, axis=dim), axis, backward)
        block = jnp.concatenate([low, block, high], axis=dim)
    return block


def unrotate(vectors, field):
    return jnp.einsum("imn,imc->inc", vectors, field, precision=lax.Precision.HIGHEST)


def rotate(vectors, field):
    return jnp.einsum("inm,imc->inc", vectors, field, precision=lax.Precision.HIGHEST)


def shifted_inverse(vectors, values, field, real_part, imag_part):
    width = field.shape[-1] // 2
    spun = unrotate(vectors, field)
    offset = real_part - values
    denom = offset * offset + imag_part * imag_part
    scale_re = (offset / denom)[..., None]
    scale_im = (-imag_part / denom)[..., None]
    first = spun[..., :width]
    second = spun[..., width:]
    mixed = jnp.concatenate(
        [scale_re * first - scale_im * second, scale_re * second + scale_im * first], axis=-1
    )
    return rotate(vectors, mixed)


def diagonal_part(vectors, values, field):
    return rotate(vectors, values[..., None] * unrotate(vectors, field))


def coupled(near_blocks, couplings):
    return jnp.einsum("iknm,ikmc->inc", couplings, near_blocks, precision=lax.Precision.HIGHEST)


def product(left, right):
    return jnp.dot(left, right, precision=lax.Precision.HIGHEST)


def per_device(neighbours, couplings, eigvectors, eigvalues, start_block):
    blk_dev, blk = eigvalues.shape
    ncol = start_block.shape[1]
    rows_here = blk_dev * blk
    total = rows_here * lax.axis_size("rows")
    count = lax.axis_size("shift")
    angle = jnp.pi * (lax.axis_index("shift").astype(jnp.float32) + 0.5) / count
    real_part = radius * jnp.cos(angle)
    imag_part = radius * jnp.sin(angle)
    local_index = neighbours - (lax.axis_index("rows") * blk_dev - blk_dev)

    def operate_on(field, padded):
        blocks_all = padded.reshape(3 * blk_dev, blk, padded.shape[-1])
        near = blocks_all[local_index]
        return diagonal_part(eigvectors, eigvalues, field) + coupled(near, couplings)

    blocks_b = start_block.reshape(blk_dev, blk, ncol)
    rhs = jnp.concatenate([blocks_b, jnp.zeros_like(blocks_b)], axis=-1)
    iterate = damping * shifted_inverse(eigvectors, eigvalues, rhs, real_part, imag_part)
    for sweep in range(1, SWEEPS):
        first = iterate[..., :ncol]
        second = iterate[..., ncol:]
        shifted = jnp.concatenate(
            [real_part * first - imag_part * second, imag_part * first + real_part * second],
            axis=-1,
        )
        iterate_padded = extended(iterate.reshape(rows_here, 2 * ncol), (("rows", 0),), rows_here)
        resid = rhs - shifted + operate_on(iterate, iterate_padded)
        iterate = iterate + damping * shifted_inverse(
            eigvectors, eigvalues, resid, real_part, imag_part
        )
    contrib = real_part / count * iterate[..., :ncol] - imag_part / count * iterate[..., ncol:]
    contrib = contrib.reshape(rows_here, ncol)
    field = lax.psum(contrib, "shift")
    gram = lax.psum(product(field.T, field), "rows") / total
    factor = jnp.linalg.cholesky(gram)
    basis = jax.scipy.linalg.solve_triangular(factor, field.T, lower=True).T
    padded = extended(basis, (("rows", 0),), rows_here)
    image = operate_on(basis.reshape(blk_dev, blk, ncol), padded).reshape(rows_here, ncol)
    projected = lax.psum(product(basis.T, image), "rows") / total
    basis_image, projected = (image, projected)
    return (basis, basis_image, projected)


def solution(mesh):
    in_specs = (
        P("rows", None),
        P("rows", None, None, None),
        P("rows", None, None),
        P("rows", None),
        P("rows", None),
    )
    out_specs = (P("rows", None), P("rows", None), P())
    return jax.shard_map(
        per_device, mesh=mesh, in_specs=in_specs, out_specs=out_specs, check_vma=False
    )
```

profile of v0, /device:TPU:2, one launch (start us, length us, event | category | flops | bytes accessed | tf_op | source)
XLA Modules:
  0.0 556.1 jit_solution(6460307151305128019)
XLA Ops:
  7.4 1.2 copy.20
  8.7 1.0 fusion.2
  9.6 0.7 fusion.32
  10.3 0.1 multiply_subtract_fusion.4
  10.5 1.1 convolution_multiply_fusion.4
  11.6 1.3 copy.23
  12.9 4.8 collective-permute-start
  17.7 1.3 collective-permute-start.1
  19.0 0.1 reshape.57
  19.1 1.1 multiply_subtract_fusion.3
  20.2 1.1 convolution_multiply_fusion.3
  21.3 1.1 fusion.37
  22.3 17.1 %collective-permute-done = f32[1024,256]{1,0:T(8,128)} collective-permute-done((f32[1024,256]{1,0:T(8,128)}, f32[1024,256]{1,0:T(8,128)}, u32[]{:S(2)}, u32[]{:S(2)}) %collective-permute-start) | collective-permute-done | bytes 1048608 | tf_op jit(solution)/shard_map/ppermute | solution.py:16
  39.4 5.1 collective-permute-done.1
  44.5 3.8 pad_maximum_fusion
  48.3 6.2 %gather_fusion = f32[64,128,256]{2,1,0:T(8,128)} fusion(f32[24,128,256]{2,1,0:T(8,128)} %bitcast.105, s32[1024]{0:T(1024)S(1)} %pad_clamp_fusion), kind=kCustom, calls=%fused_computation | custom fusion | bytes 16777472 | tf_op jit(solution)/shard_map/gather | solution.py:72
  54.5 17.7 %fusion.11 = f32[8,128,256]{1,2,0:T(8,128)S(1)} fusion(f32[8,256,128]{2,1,0:T(8,128)S(1)} %fusion.37, f32[8,8,128,256]{3,2,1,0:T(8,128)} %bitcast.108, f32[8,8,128,128]{3,2,1,0:T(8,128)} %param.6, f32[8,128,128]{1,2,0:T(8,128)S(1)} %copy.20, f32[8,128,128]{1,2,0:T(8,128)} %get-tuple-element.18, f32[8,128,128]{1,2,0:T(8,128)} %get-tuple-element.17), kind=kOutput, calls=%fused_computation.26 | convolution fusion | flops 3222274048 | bytes 16252928 | tf_op jit(solution)/shard_map/iknm,ikmc->inc/dot_general | solution.py:52
  72.2 1.1 convolution_bitcast_fusion.3
  73.2 0.1 multiply_subtract_fusion.2
  73.4 1.1 fusion.8
  74.5 1.3 copy.26
  75.8 4.0 collective-permute-start.2
  79.8 1.3 collective-permute-start.3
  81.1 1.1 multiply_subtract_fusion.1
  82.2 1.1 convolution_multiply_fusion.1
  83.3 1.1 fusion.38
  84.3 16.2 %collective-permute-done.2 = f32[1024,256]{1,0:T(8,128)} collective-permute-done((f32[1024,256]{1,0:T(8,128)}, f32[1024,256]{1,0:T(8,128)}, u32[]{:S(2)}, u32[]{:S(2)}) %collective-permute-start.2) | collective-permute-done | bytes 1048608 | tf_op jit(solution)/shard_map/ppermute | solution.py:16
  100.6 5.6 %collective-permute-done.3 = f32[1024,256]{1,0:T(8,128)} collective-permute-done((f32[1024,256]{1,0:T(8,128)}, f32[1024,256]{1,0:T(8,128)}, u32[]{:S(2)}, u32[]{:S(2)}) %collective-permute-start.3) | collective-permute-done | bytes 1048608 | tf_op jit(solution)/shard_map/ppermute | solution.py:19
  106.2 3.8 pad_maximum_fusion.1
  110.0 6.2 %gather_fusion.1 = f32[64,128,256]{2,1,0:T(8,128)} fusion(f32[24,128,256]{2,1,0:T(8,128)} %bitcast.106, s32[1024]{0:T(1024)S(1)} %pad_clamp_fusion), kind=kCustom, calls=%fused_computation.1 | custom fusion | bytes 16777472 | tf_op jit(solution)/shard_map/gather | solution.py:72
  116.2 17.3 %fusion.14 = f32[8,128,256]{1,2,0:T(8,128)S(1)} fusion(f32[8,256,128]{2,1,0:T(8,128)S(1)} %fusion.38, f32[8,8,128,256]{3,2,1,0:T(8,128)} %bitcast.107, f32[8,8,128,128]{3,2,1,0:T(8,128)} %param.6, f32[8,128,128]{1,2,0:T(8,128)S(1)} %copy.20, f32[8,128,128]{1,2,0:T(8,128)} %get-tuple-element.16, f32[8,128,128]{1,2,0:T(8,128)} %get-tuple-element.15), kind=kOutput, calls=%fused_computation.29 | convolution fusion | flops 3222274048 | bytes 16252928 | tf_op jit(solution)/shard_map/iknm,ikmc->inc/dot_general | solution.py:52
  133.5 1.1 convolution_bitcast_fusion.2
  134.6 0.1 multiply_subtract_fusion
  134.7 1.1 fusion.6
  135.8 0.1 fusion.26
  135.9 1.0 copy.29
  136.9 0.0 all-reduce.7.cloned.1.call-start
  137.0 65.0 %all-reduce.5.cloned.1.call-done = f32[1024,128]{1,0:T(8,128)} async-done(((f32[1024,128]{1,0:T(8,128)}), f32[1024,128]{1,0:T(8,128)}) %all-reduce.5.cloned.1.call-update) | async-done | bytes 524304 | tf_op jit(solution)/shard_map/psum | solution.py:92
  202.0 2.8 fusion.39
  204.8 0.3 all-reduce.9.cloned.1.call-start
  205.1 143.7 %all-reduce.7.cloned.1.call-done = f32[128,128]{0,1:T(8,128)} async-done(((f32[128,128]{0,1:T(8,128)}), f32[128,128]{0,1:T(8,128)}) %all-reduce.7.cloned.1.call-update) | async-done | bytes 65552 | tf_op jit(solution)/shard_map/psum | solution.py:93
  348.7 0.8 broadcast_multiply_fusion.1
  349.6 0.1 copy.31
  349.7 0.9 fusion.30
  350.5 11.7 %cholesky.16 = f32[128,128]{1,0:T(8,128)S(1)} custom-call(f32[128,128]{1,0:T(8,128)S(1)} %fusion.30), custom_call_target="Cholesky" | custom-call | tf_op jit(solution)/shard_map/jit(cholesky)/cholesky | solution.py:94
  362.3 0.6 compare_reduce_fusion
  362.9 0.7 fusion.27
  363.6 9.8 %custom-call.7 = f32[1,128,128]{1,2,0:T(8,128)S(1)} custom-call(f32[1,128,128]{2,1,0:T(8,128)S(1)} %fusion.27), custom_call_target="InvertDiagBlocksLowerTriangular" | custom-call | tf_op jit(solution)/shard_map/jit(_solve_triangular)/triangular_solve | solution.py:95
  373.4 1.7 fusion.28
  375.1 3.2 collective-permute-start.4
  378.3 1.5 collective-permute-start.5
  379.9 0.6 convolution_multiply_fusion.5
  380.5 4.7 collective-permute-done.4
  385.2 4.2 collective-permute-done.5
  389.4 1.3 pad_maximum_fusion.2
  390.6 1.9 copy.48
  392.5 2.8 gather_fusion.2
  395.3 8.1 %convolution_bitcast_fusion.4 = f32[8,128,128]{1,2,0:T(8,128)S(1)} fusion(f32[8,8,128,128]{3,2,1,0:T(8,128)} %bitcast.112, f32[8,8,128,128]{3,2,1,0:T(8,128)} %param.6), kind=kOutput, calls=%fused_computation.30 | convolution fusion | flops 1610612736 | bytes 8912896 | tf_op jit(solution)/shard_map/iknm,ikmc->inc/dot_general | solution.py:52
  403.4 1.2 convolution_add_fusion
  404.6 1.6 fusion.40
  406.2 1.0 copy.34
  407.2 140.5 %all-reduce.9.cloned.1.call-done = f32[128,128]{0,1:T(8,128)} async-done(((f32[128,128]{0,1:T(8,128)}), f32[128,128]{0,1:T(8,128)}) %all-reduce.9.cloned.1.call-update) | async-done | bytes 65552 | tf_op jit(solution)/shard_map/psum | solution.py:98
  547.7 0.8 broadcast_multiply_fusion
  548.6 0.7 copy.35
  (15 shorter events, 0.2 us)
Async XLA Ops:
  7.2 1.5 copy-start
  7.2 194.8 %all-reduce.5.cloned.1.call-start = ((), (), s32[]{:S(2)}) async-start(), calls=%async_computation | async-start | bytes 1048576 | tf_op jit(solution)/shard_map/psum | solution.py:92
  8.6 10.3 %copy-start.3 = (s32[8,8]{1,0:T(8,128)S(1)}, s32[8,8]{1,0:T(8,128)}, u32[]{:S(2)}) copy-start(s32[8,8]{1,0:T(8,128)} %param.5) | copy-start | bytes 772
  10.3 9.9 %copy-start.2 = (f32[8,128]{1,0:T(8,128)S(1)}, f32[8,128]{1,0:T(8,128)}, u32[]{:S(2)}) copy-start(f32[8,128]{1,0:T(8,128)} %param.8) | copy-start | bytes 12292
  12.9 26.5 %collective-permute-start = (f32[1024,256]{1,0:T(8,128)}, f32[1024,256]{1,0:T(8,128)}, u32[]{:S(2)}, u32[]{:S(2)}) collective-permute-start(f32[1024,256]{1,0:T(8,128)} %bitcast.3), channel_id=1, source_target_pairs={{0,1},{1,2},{2,3},{3,4},{4,5},{5,6},{6,7},{7,8},{8,9},{9,10},{10,1... | collective-permute-start | bytes 3145736 | tf_op jit(solution)/shard_map/ppermute | solution.py:16
  17.7 26.8 %collective-permute-start.1 = (f32[1024,256]{1,0:T(8,128)}, f32[1024,256]{1,0:T(8,128)}, u32[]{:S(2)}, u32[]{:S(2)}) collective-permute-start(f32[1024,256]{1,0:T(8,128)} %bitcast.3), channel_id=1, source_target_pairs={{1,0},{2,1},{3,2},{4,3},{5,4},{6,5},{7,6},{8,7},{9,8},{10,9},{11,1... | collective-permute-start | bytes 3145736 | tf_op jit(solution)/shard_map/ppermute | solution.py:19
  75.8 24.8 %collective-permute-start.2 = (f32[1024,256]{1,0:T(8,128)}, f32[1024,256]{1,0:T(8,128)}, u32[]{:S(2)}, u32[]{:S(2)}) collective-permute-start(f32[1024,256]{1,0:T(8,128)} %bitcast.11), channel_id=1, source_target_pairs={{0,1},{1,2},{2,3},{3,4},{4,5},{5,6},{6,7},{7,8},{8,9},{9,10},{10,1... | collective-permute-start | bytes 3145736 | tf_op jit(solution)/shard_map/ppermute | solution.py:16
  79.8 26.4 %collective-permute-start.3 = (f32[1024,256]{1,0:T(8,128)}, f32[1024,256]{1,0:T(8,128)}, u32[]{:S(2)}, u32[]{:S(2)}) collective-permute-start(f32[1024,256]{1,0:T(8,128)} %bitcast.11), channel_id=1, source_target_pairs={{1,0},{2,1},{3,2},{4,3},{5,4},{6,5},{7,6},{8,7},{9,8},{10,9},{11,1... | collective-permute-start | bytes 3145736 | tf_op jit(solution)/shard_map/ppermute | solution.py:19
  136.9 211.8 %all-reduce.7.cloned.1.call-start = ((), (), s32[]{:S(2)}) async-start(), calls=%async_computation.1 | async-start | bytes 131072 | tf_op jit(solution)/shard_map/psum | solution.py:93
  204.8 342.9 %all-reduce.9.cloned.1.call-start = ((), (), s32[]{:S(2)}) async-start(), calls=%async_computation.2 | async-start | bytes 131072 | tf_op jit(solution)/shard_map/psum | solution.py:98
  375.1 10.1 %collective-permute-start.4 = (f32[1024,128]{0,1:T(8,128)S(1)}, f32[1024,128]{0,1:T(8,128)S(1)}, u32[]{:S(2)}, u32[]{:S(2)}) collective-permute-start(f32[1024,128]{0,1:T(8,128)S(1)} %bitcast.113), channel_id=1, source_target_pairs={{0,1},{1,2},{2,3},{3,4},{4,5},{5,6},{6,7},{7,8},{8,9},{9,10},{10,1... | collective-permute-start | bytes 1572872 | tf_op jit(solution)/shard_map/ppermute | solution.py:16
  378.3 11.1 %collective-permute-start.5 = (f32[1024,128]{0,1:T(8,128)S(1)}, f32[1024,128]{0,1:T(8,128)S(1)}, u32[]{:S(2)}, u32[]{:S(2)}) collective-permute-start(f32[1024,128]{0,1:T(8,128)S(1)} %bitcast.114), channel_id=1, source_target_pairs={{1,0},{2,1},{3,2},{4,3},{5,4},{6,5},{7,6},{8,7},{9,8},{10,9},{11,1... | collective-permute-start | bytes 1572872 | tf_op jit(solution)/shard_map/ppermute | solution.py:19
  404.6 144.7 %copy-start.1 = (f32[8,128,128]{1,2,0:T(8,128)}, f32[8,128,128]{1,2,0:T(8,128)S(1)}, u32[]{:S(2)}) copy-start(f32[8,128,128]{1,2,0:T(8,128)S(1)} %convolution_add_fusion) | copy-start | bytes 1572868
Sparse Core Ops, SparseCore 0:
  137.1 64.8 all-reduce.4
  206.0 142.7 all-reduce.6
  406.4 141.3 all-reduce.8
where the time goes:
time: 562 us; the launch traced here: 556 us
  waiting for transfers between devices  402 us (72%)
  matrix products  61.7 us (11%)
  other arithmetic  37.6 us (7%)
  local copies, waits for them, and re-layouts  23.8 us (4%)
  starting transfers between devices  16.5 us (3%)
  between operations  14.5 us (3%)
    psum x1, waiting for transfers between devices, per_device(): gram = lax.psum(product(field.T, field), 'rows') / total  144 us
    psum x1, waiting for transfers between devices, per_device(): projected = lax.psum(product(basis.T, image), 'rows') / total  140 us
    psum x1, waiting for transfers between devices, per_device(): field = lax.psum(contrib, 'shift')  65 us
    dot_general x3, matrix products, coupled(): jnp.einsum('iknm,ikmc->inc', couplings, near_blocks, precision=lax.Precis...  43.1 us
    ppermute x3, waiting for transfers between devices, extended(): lax.ppermute(lax.slice_in_dim(block, block.shape[dim] - width, None, axis...  38 us
    gather x3, local copies, waits for them, and re-layouts, operate_on(): near = blocks_all[local_index]  15.2 us
    ppermute x3, waiting for transfers between devices, extended(): lax.ppermute(lax.slice_in_dim(block, 0, width, axis=dim), axis, backward)  14.9 us
    another operation x3, other arithmetic, per_device(): factor = jnp.linalg.cholesky(gram)  12.4 us
  transfers between devices with their start and end apart: 9, of which 9 were waited for; matrix products, arithmetic and copies ran while one was open for 1% of the time, Pallas kernels for 0%

commit v1 on v0

--- a/solution.py
+++ b/solution.py
@@ -6,6 +6,15 @@
 SWEEPS = 3
 radius = 1.0
 damping = 0.8
+
+
+def sum_by_hops(x, name):
+    count = lax.axis_size(name)
+    total, far = (x, 1)
+    while far < count:
+        total = total + lax.ppermute(total, name, [(i, i ^ far) for i in range(count)])
+        far = 2 * far
+    return total
 
 
 def extended(block, sides, width):
@@ -89,7 +98,7 @@
         )
     contrib = real_part / count * iterate[..., :ncol] - imag_part / count * iterate[..., ncol:]
     contrib = contrib.reshape(rows_here, ncol)
-    field = lax.psum(contrib, "shift")
+    field = sum_by_hops(contrib, "shift")
     gram = lax.psum(product(field.T, field), "rows") / total
     factor = jnp.linalg.cholesky(gram)
     basis = jax.scipy.linalg.solve_triangular(factor, field.T, lower=True).T

time: 562 us -> 523 us (0.931)
  waiting for transfers between devices: 402 us -> 364 us
    psum x1 -> x0, waiting for transfers between devices: 65 us -> none  [per_device(): field = lax.psum(contrib, 'shift')]
    ppermute x0 -> x3, waiting for transfers between devices: none -> 27.8 us  [sum_by_hops(): lax.ppermute(total, name, [(i, i ^ far) for i in range(count)])]
  transfers between devices with their start and end apart: 9 -> 11, of which waited for: 9 -> 11; matrix products, arithmetic and copies ran while one was open for 1% -> 2% of each run, Pallas kernels for 0% -> 0%
where the time goes in v1:
time: 523 us; the launch traced here: 518 us
  waiting for transfers between devices  364 us (70%)
  matrix products  59.4 us (11%)
  other arithmetic  37.8 us (7%)
  local copies, waits for them, and re-layouts  23 us (4%)
  starting transfers between devices  19.3 us (4%)
  between operations  14.8 us (3%)
    psum x1, waiting for transfers between devices, per_device(): gram = lax.psum(product(field.T, field), 'rows') / total  142 us
    psum x1, waiting for transfers between devices, per_device(): projected = lax.psum(product(basis.T, image), 'rows') / total  141 us
    dot_general x3, matrix products, coupled(): jnp.einsum('iknm,ikmc->inc', couplings, near_blocks, precision=lax.Precis...  43.1 us
    ppermute x3, waiting for transfers between devices, extended(): lax.ppermute(lax.slice_in_dim(block, block.shape[dim] - width, None, axis...  38.1 us
    ppermute x3, waiting for transfers between devices, sum_by_hops(): lax.ppermute(total, name, [(i, i ^ far) for i in range(count)])  27.8 us
    gather x3, local copies, waits for them, and re-layouts, operate_on(): near = blocks_all[local_index]  15.2 us
    ppermute x3, waiting for transfers between devices, extended(): lax.ppermute(lax.slice_in_dim(block, 0, width, axis=dim), axis, backward)  14.8 us
    another operation x3, other arithmetic, per_device(): factor = jnp.linalg.cholesky(gram)  12.4 us
  transfers between devices with their start and end apart: 11, of which 11 were waited for; matrix products, arithmetic and copies ran while one was open for 2% of the time, Pallas kernels for 0%

profile of v1, /device:TPU:2, one launch (start us, length us, event | category | flops | bytes accessed | tf_op | source)
XLA Modules:
  0.0 518.0 jit_solution(1652321847701035332)
XLA Ops:
  7.4 1.2 copy.20
  8.7 1.0 fusion.2
  9.6 0.7 fusion.32
  10.3 0.1 multiply_subtract_fusion.4
  10.5 1.1 convolution_multiply_fusion.4
  11.6 1.3 copy.23
  12.9 4.8 collective-permute-start
  17.7 1.3 collective-permute-start.1
  19.1 1.1 multiply_subtract_fusion.3
  20.2 1.1 convolution_multiply_fusion.3
  21.2 1.1 fusion.37
  22.3 17.1 %collective-permute-done = f32[1024,256]{1,0:T(8,128)} collective-permute-done((f32[1024,256]{1,0:T(8,128)}, f32[1024,256]{1,0:T(8,128)}, u32[]{:S(2)}, u32[]{:S(2)}) %collective-permute-start) | collective-permute-done | bytes 1048608 | tf_op jit(solution)/shard_map/ppermute | solution.py:25
  39.4 5.1 collective-permute-done.1
  44.5 3.8 pad_maximum_fusion
  48.2 6.2 %gather_fusion = f32[64,128,256]{2,1,0:T(8,128)} fusion(f32[24,128,256]{2,1,0:T(8,128)} %bitcast.106, s32[1024]{0:T(1024)S(1)} %pad_clamp_fusion), kind=kCustom, calls=%fused_computation | custom fusion | bytes 16777472 | tf_op jit(solution)/shard_map/gather | solution.py:81
  54.4 17.7 %fusion.11 = f32[8,128,256]{1,2,0:T(8,128)S(1)} fusion(f32[8,256,128]{2,1,0:T(8,128)S(1)} %fusion.37, f32[8,8,128,256]{3,2,1,0:T(8,128)} %bitcast.109, f32[8,8,128,128]{3,2,1,0:T(8,128)} %param.6, f32[8,128,128]{1,2,0:T(8,128)S(1)} %copy.20, f32[8,128,128]{1,2,0:T(8,128)} %get-tuple-element.18, f32[8,128,128]{1,2,0:T(8,128)} %get-tuple-element.17), kind=kOutput, calls=%fused_computation.26 | convolution fusion | flops 3222274048 | bytes 16252928 | tf_op jit(solution)/shard_map/iknm,ikmc->inc/dot_general | solution.py:61
  72.1 1.1 convolution_bitcast_fusion.3
  73.2 0.1 multiply_subtract_fusion.2
  73.3 1.1 fusion.8
  74.4 1.3 copy.26
  75.8 4.0 collective-permute-start.2
  79.8 1.3 collective-permute-start.3
  81.1 1.1 multiply_subtract_fusion.1
  82.2 1.1 convolution_multiply_fusion.1
  83.2 1.1 fusion.38
  84.3 16.3 %collective-permute-done.2 = f32[1024,256]{1,0:T(8,128)} collective-permute-done((f32[1024,256]{1,0:T(8,128)}, f32[1024,256]{1,0:T(8,128)}, u32[]{:S(2)}, u32[]{:S(2)}) %collective-permute-start.2) | collective-permute-done | bytes 1048608 | tf_op jit(solution)/shard_map/ppermute | solution.py:25
  100.6 5.6 %collective-permute-done.3 = f32[1024,256]{1,0:T(8,128)} collective-permute-done((f32[1024,256]{1,0:T(8,128)}, f32[1024,256]{1,0:T(8,128)}, u32[]{:S(2)}, u32[]{:S(2)}) %collective-permute-start.3) | collective-permute-done | bytes 1048608 | tf_op jit(solution)/shard_map/ppermute | solution.py:28
  106.2 3.8 pad_maximum_fusion.1
  109.9 6.2 %gather_fusion.1 = f32[64,128,256]{2,1,0:T(8,128)} fusion(f32[24,128,256]{2,1,0:T(8,128)} %bitcast.107, s32[1024]{0:T(1024)S(1)} %pad_clamp_fusion), kind=kCustom, calls=%fused_computation.1 | custom fusion | bytes 16777472 | tf_op jit(solution)/shard_map/gather | solution.py:81
  116.1 17.3 %fusion.14 = f32[8,128,256]{1,2,0:T(8,128)S(1)} fusion(f32[8,256,128]{2,1,0:T(8,128)S(1)} %fusion.38, f32[8,8,128,256]{3,2,1,0:T(8,128)} %bitcast.108, f32[8,8,128,128]{3,2,1,0:T(8,128)} %param.6, f32[8,128,128]{1,2,0:T(8,128)S(1)} %copy.20, f32[8,128,128]{1,2,0:T(8,128)} %get-tuple-element.16, f32[8,128,128]{1,2,0:T(8,128)} %get-tuple-element.15), kind=kOutput, calls=%fused_computation.29 | convolution fusion | flops 3222274048 | bytes 16252928 | tf_op jit(solution)/shard_map/iknm,ikmc->inc/dot_general | solution.py:61
  133.5 1.1 convolution_bitcast_fusion.2
  134.5 0.1 multiply_subtract_fusion
  134.7 1.1 fusion.6
  135.9 0.2 copy.29
  136.1 0.1 collective-permute-start.4
  136.2 1.9 collective-permute-done.4
  138.2 0.6 collective-permute-start.5
  138.8 13.4 %collective-permute-done.5 = f32[1024,128]{1,0:T(8,128)S(1)} collective-permute-done((f32[1024,128]{1,0:T(8,128)S(1)}, f32[1024,128]{1,0:T(8,128)S(1)}, u32[]{:S(2)}, u32[]{:S(2)}) %collective-permute-start.5) | collective-permute-done | bytes 524320 | tf_op jit(solution)/shard_map/ppermute | solution.py:15
  152.3 2.4 collective-permute-start.6
  154.7 12.5 %collective-permute-done.6 = f32[1024,128]{1,0:T(8,128)S(1)} collective-permute-done((f32[1024,128]{1,0:T(8,128)S(1)}, f32[1024,128]{1,0:T(8,128)S(1)}, u32[]{:S(2)}, u32[]{:S(2)}) %collective-permute-start.6) | collective-permute-done | bytes 524320 | tf_op jit(solution)/shard_map/ppermute | solution.py:15
  167.2 1.6 fusion.39
  168.9 142.4 %all-reduce.4.cloned.1.call-done = f32[128,128]{0,1:T(8,128)} async-done(((f32[128,128]{0,1:T(8,128)}), f32[128,128]{0,1:T(8,128)}) %all-reduce.4.cloned.1.call-update) | async-done | bytes 65552 | tf_op jit(solution)/shard_map/psum | solution.py:102
  311.4 0.8 broadcast_multiply_fusion.1
  312.3 0.9 fusion.30
  313.2 11.7 %cholesky.16 = f32[128,128]{1,0:T(8,128)S(1)} custom-call(f32[128,128]{1,0:T(8,128)S(1)} %fusion.30), custom_call_target="Cholesky" | custom-call | tf_op jit(solution)/shard_map/jit(cholesky)/cholesky | solution.py:103
  324.9 0.6 compare_reduce_fusion
  325.6 0.7 fusion.27
  326.2 9.8 %custom-call.7 = f32[1,128,128]{1,2,0:T(8,128)S(1)} custom-call(f32[1,128,128]{2,1,0:T(8,128)S(1)} %fusion.27), custom_call_target="InvertDiagBlocksLowerTriangular" | custom-call | tf_op jit(solution)/shard_map/jit(_solve_triangular)/triangular_solve | solution.py:104
  336.0 0.6 fusion.28
  336.7 3.2 collective-permute-start.7
  339.9 1.5 collective-permute-start.8
  341.5 0.6 convolution_multiply_fusion.5
  342.1 4.7 collective-permute-done.7
  346.8 4.2 collective-permute-done.8
  351.0 1.3 pad_maximum_fusion.2
  352.2 1.9 copy.48
  354.1 2.8 gather_fusion.2
  356.9 8.1 %convolution_bitcast_fusion.4 = f32[8,128,128]{1,2,0:T(8,128)S(1)} fusion(f32[8,8,128,128]{3,2,1,0:T(8,128)} %bitcast.113, f32[8,8,128,128]{3,2,1,0:T(8,128)} %param.6), kind=kOutput, calls=%fused_computation.30 | convolution fusion | flops 1610612736 | bytes 8912896 | tf_op jit(solution)/shard_map/iknm,ikmc->inc/dot_general | solution.py:61
  365.0 1.2 convolution_add_fusion
  366.2 1.6 fusion.40
  367.8 1.0 copy.34
  368.8 140.5 %all-reduce.6.cloned.1.call-done = f32[128,128]{0,1:T(8,128)} async-done(((f32[128,128]{0,1:T(8,128)}), f32[128,128]{0,1:T(8,128)}) %all-reduce.6.cloned.1.call-update) | async-done | bytes 65552 | tf_op jit(solution)/shard_map/psum | solution.py:107
  509.3 0.8 broadcast_multiply_fusion
  510.2 0.7 copy.35
  (21 shorter events, 0.6 us)
Async XLA Ops:
  7.2 1.5 copy-start
  7.2 304.2 %all-reduce.4.cloned.1.call-start = ((), (), s32[]{:S(2)}) async-start(), calls=%async_computation | async-start | bytes 131072 | tf_op jit(solution)/shard_map/psum | solution.py:102
  8.6 10.3 %copy-start.3 = (s32[8,8]{1,0:T(8,128)S(1)}, s32[8,8]{1,0:T(8,128)}, u32[]{:S(2)}) copy-start(s32[8,8]{1,0:T(8,128)} %param.5) | copy-start | bytes 772
  10.3 9.8 %copy-start.2 = (f32[8,128]{1,0:T(8,128)S(1)}, f32[8,128]{1,0:T(8,128)}, u32[]{:S(2)}) copy-start(f32[8,128]{1,0:T(8,128)} %param.8) | copy-start | bytes 12292
  12.9 26.5 %collective-permute-start = (f32[1024,256]{1,0:T(8,128)}, f32[1024,256]{1,0:T(8,128)}, u32[]{:S(2)}, u32[]{:S(2)}) collective-permute-start(f32[1024,256]{1,0:T(8,128)} %bitcast.3), channel_id=1, source_target_pairs={{0,1},{1,2},{2,3},{3,4},{4,5},{5,6},{6,7},{7,8},{8,9},{9,10},{10,1... | collective-permute-start | bytes 3145736 | tf_op jit(solution)/shard_map/ppermute | solution.py:25
  17.7 26.8 %collective-permute-start.1 = (f32[1024,256]{1,0:T(8,128)}, f32[1024,256]{1,0:T(8,128)}, u32[]{:S(2)}, u32[]{:S(2)}) collective-permute-start(f32[1024,256]{1,0:T(8,128)} %bitcast.3), channel_id=1, source_target_pairs={{1,0},{2,1},{3,2},{4,3},{5,4},{6,5},{7,6},{8,7},{9,8},{10,9},{11,1... | collective-permute-start | bytes 3145736 | tf_op jit(solution)/shard_map/ppermute | solution.py:28
  75.8 24.8 %collective-permute-start.2 = (f32[1024,256]{1,0:T(8,128)}, f32[1024,256]{1,0:T(8,128)}, u32[]{:S(2)}, u32[]{:S(2)}) collective-permute-start(f32[1024,256]{1,0:T(8,128)} %bitcast.11), channel_id=1, source_target_pairs={{0,1},{1,2},{2,3},{3,4},{4,5},{5,6},{6,7},{7,8},{8,9},{9,10},{10,1... | collective-permute-start | bytes 3145736 | tf_op jit(solution)/shard_map/ppermute | solution.py:25
  79.8 26.4 %collective-permute-start.3 = (f32[1024,256]{1,0:T(8,128)}, f32[1024,256]{1,0:T(8,128)}, u32[]{:S(2)}, u32[]{:S(2)}) collective-permute-start(f32[1024,256]{1,0:T(8,128)} %bitcast.11), channel_id=1, source_target_pairs={{1,0},{2,1},{3,2},{4,3},{5,4},{6,5},{7,6},{8,7},{9,8},{10,9},{11,1... | collective-permute-start | bytes 3145736 | tf_op jit(solution)/shard_map/ppermute | solution.py:28
  136.1 2.0 collective-permute-start.4
  138.2 14.1 %collective-permute-start.5 = (f32[1024,128]{1,0:T(8,128)S(1)}, f32[1024,128]{1,0:T(8,128)S(1)}, u32[]{:S(2)}, u32[]{:S(2)}) collective-permute-start(f32[1024,128]{1,0:T(8,128)S(1)} %bitcast_add_fusion.1), channel_id=1, source_target_pairs={{0,64},{32,96},{64,0},{96,32},{128,192},{160,224},{192,128},{224,1... | collective-permute-start | bytes 1572872 | tf_op jit(solution)/shard_map/ppermute | solution.py:15
  152.3 14.9 %collective-permute-start.6 = (f32[1024,128]{1,0:T(8,128)S(1)}, f32[1024,128]{1,0:T(8,128)S(1)}, u32[]{:S(2)}, u32[]{:S(2)}) collective-permute-start(f32[1024,128]{1,0:T(8,128)S(1)} %add.109), channel_id=1, source_target_pairs={{0,128},{32,160},{64,192},{96,224},{128,0},{160,32},{192,64},{224,... | collective-permute-start | bytes 1572872 | tf_op jit(solution)/shard_map/ppermute | solution.py:15
  168.9 340.4 %all-reduce.6.cloned.1.call-start = ((), (), s32[]{:S(2)}) async-start(), calls=%async_computation.1 | async-start | bytes 131072 | tf_op jit(solution)/shard_map/psum | solution.py:107
  336.7 10.1 %collective-permute-start.7 = (f32[1024,128]{0,1:T(8,128)S(1)}, f32[1024,128]{0,1:T(8,128)S(1)}, u32[]{:S(2)}, u32[]{:S(2)}) collective-permute-start(f32[1024,128]{0,1:T(8,128)S(1)} %bitcast.114), channel_id=1, source_target_pairs={{0,1},{1,2},{2,3},{3,4},{4,5},{5,6},{6,7},{7,8},{8,9},{9,10},{10,1... | collective-permute-start | bytes 1572872 | tf_op jit(solution)/shard_map/ppermute | solution.py:25
  339.9 11.1 %collective-permute-start.8 = (f32[1024,128]{0,1:T(8,128)S(1)}, f32[1024,128]{0,1:T(8,128)S(1)}, u32[]{:S(2)}, u32[]{:S(2)}) collective-permute-start(f32[1024,128]{0,1:T(8,128)S(1)} %bitcast.115), channel_id=1, source_target_pairs={{1,0},{2,1},{3,2},{4,3},{5,4},{6,5},{7,6},{8,7},{9,8},{10,9},{11,1... | collective-permute-start | bytes 1572872 | tf_op jit(solution)/shard_map/ppermute | solution.py:28
  366.2 144.7 %copy-start.1 = (f32[8,128,128]{1,2,0:T(8,128)}, f32[8,128,128]{1,2,0:T(8,128)S(1)}, u32[]{:S(2)}) copy-start(f32[8,128,128]{1,2,0:T(8,128)S(1)} %convolution_add_fusion) | copy-start | bytes 1572868
Sparse Core Ops, SparseCore 0:
  169.0 142.3 all-reduce.3
  368.0 141.3 all-reduce.5
